TPU v7x, 32 devices: a whole 2x2x4 slice. The times are simulated.
32 devices in a mesh: seq: 16 (over z, y, x), head: 2 (over core).
Axes of the slice: x: 2, y: 2, z: 4, core: 2. Of those that a mesh axis runs over, the one named last changes fastest.
Arguments:
- queries: bfloat16 [4096, 5120], P('seq', 'head'), may hold values from -100 to 100
- keys: bfloat16 [4096, 5120], P('seq', 'head'), may hold values from -12 to 12
- values: bfloat16 [4096, 5120], P('seq', 'head'), may hold values from -6 to 6
- hidden: bfloat16 [4096, 5120], P('seq', 'head'), may hold values from -3 to 3
- cached: bfloat16 [4096, 5120], P('seq', 'head'), may hold values from -6 to 6
- active: int32 [4096], P('seq'), may hold values from 0 to 1, as said below
- w_out: bfloat16 [5120, 5120], P('head', 'seq'), may hold values from -0.078125 to 0.078125
Outputs:
- block_output: bfloat16 [4096, 5120], P('seq', 'head')
Inputs may be any that keep to these rules, and one draw needn't show every extreme that they name: `active`: exactly 176 ones in all; among the 256 tokens of one index of seq at most 32 ones, and that many on some of them.
All inputs are finite; a program needn't handle non-finite values.
Results may differ from a plain program's by a relative error of at most 0.0039.
Values may be sent and summed in bfloat16 or wider, within the bound.
No kernel may reach another device: no remote copies, remote signals or barrier semaphores. Data moves between devices by JAX's collectives and lax.ppermute only.
A program may use at most 64 MiB of HBM per device.

v0:
```python
import jax
import jax.numpy as jnp
from jax import lax
from jax.sharding import PartitionSpec as P

HD = 128


def for_sending(value):

    def short(part):
        return part.astype(jnp.bfloat16) if part.dtype == jnp.float32 else part

    return jax.tree.map(short, value)


def local_partials(query_rows, keys, values):
    head_count = keys.shape[1] // HD
    inv_root = 1.0 / HD**0.5

    def one_head(head):
        start = head * HD
        q_head = lax.dynamic_slice_in_dim(query_rows, start, HD, 1)
        k_head = lax.dynamic_slice_in_dim(keys, start, HD, 1)
        v_head = lax.dynamic_slice_in_dim(values, start, HD, 1)
        scores = (
            lax.dot_general(
                q_head, k_head, (((1,), (1,)), ((), ())), preferred_element_type=jnp.float32
            )
            * inv_root
        )
        peak = jnp.max(scores, axis=1)
        expo = jnp.exp(scores - peak[:, None])
        total = jnp.sum(expo, axis=1)
        block_out = jnp.dot(expo.astype(jnp.bfloat16), v_head, preferred_element_type=jnp.float32)
        return ((block_out / total[:, None]).astype(jnp.bfloat16), peak, total)

    return lax.map(one_head, jnp.arange(head_count, dtype=jnp.int32))


def shards(queries, keys, values, hidden, cached, active, w_out):
    tok_dev, features = queries.shape
    head_count = features // HD
    devices = lax.axis_size("seq")
    capacity = tok_dev // 8
    act_rows = jnp.nonzero(active, size=capacity, fill_value=tok_dev)[0].astype(jnp.int32)
    safe_rows = jnp.minimum(act_rows, tok_dev - 1)
    own_queries = queries[safe_rows]
    gathered = lax.all_gather(own_queries, "seq", axis=0, tiled=True)
    block_out, block_peak, block_total = local_partials(gathered, keys, values)
    block_out = block_out.reshape(head_count, devices, capacity, HD)
    peak_in, total_in = (
        lax.all_to_all(
            block_peak.reshape(head_count, devices, capacity),
            "seq",
            split_axis=1,
            concat_axis=1,
            tiled=True,
        ),
        lax.all_to_all(
            block_total.reshape(head_count, devices, capacity),
            "seq",
            split_axis=1,
            concat_axis=1,
            tiled=True,
        ),
    )
    out_in = lax.all_to_all(
        for_sending(block_out), "seq", split_axis=1, concat_axis=1, tiled=True
    ).astype(block_out.dtype)
    top_max = jnp.max(peak_in, axis=1, keepdims=True)
    weight = total_in * jnp.exp(peak_in - top_max)
    mixed = jnp.einsum("hnc,hncd->hcd", weight, out_in.astype(jnp.float32))
    mixed = mixed / jnp.sum(weight, axis=1)[:, :, None]
    attn = jnp.transpose(mixed, (1, 0, 2)).reshape(capacity, features).astype(jnp.bfloat16)
    own_columns = w_out.shape[1]
    terms = jnp.dot(
        lax.all_gather(attn, "seq", axis=0, tiled=True), w_out, preferred_element_type=jnp.float32
    )
    terms = lax.psum(terms.astype(jnp.bfloat16), "head").astype(jnp.float32)
    terms = terms.reshape(devices, capacity, own_columns)
    arrived = lax.all_to_all(
        terms.astype(jnp.bfloat16), "seq", split_axis=0, concat_axis=2, tiled=True
    ).astype(terms.dtype)
    summed = lax.dynamic_slice_in_dim(arrived[0], lax.axis_index("head") * features, features, 1)
    updated = (hidden[safe_rows].astype(jnp.float32) + summed).astype(jnp.bfloat16)
    return cached.at[act_rows].set(updated, mode="drop")


def solution(mesh):
    placed = (
        P("seq", "head"),
        P("seq", "head"),
        P("seq", "head"),
        P("seq", "head"),
        P("seq", "head"),
        P("seq"),
        P("head", "seq"),
    )
    return jax.shard_map(
        shards, mesh=mesh, in_specs=placed, out_specs=P("seq", "head"), check_vma=False
    )
```

profile of v0, /device:TPU:0, one launch (start us, length us, event | category | flops | bytes accessed | tf_op | source)
XLA Modules:
  0.0 377.9 jit_solution(9547690487952534565)
XLA Ops:
  6.5 2.6 copy.57
  10.5 2.3 scatter_custom_fusion
  13.8 1.3 gather_fusion
  15.2 66.8 %all-gather.6.cloned.1.call-done = bf16[512,2560]{1,0:T(8,128)(2,1)} async-done(((bf16[32,2560]{1,0:T(8,128)(2,1)}), bf16[512,2560]{1,0:T(8,128)(2,1)}) %all-gather.6.cloned.1.call-update) | async-done | bytes 2621456 | tf_op jit(solution)/shard_map/all_gather | solution.py:49
  82.0 88.6 %while.14 = (s32[]{:T(128)}, bf16[20,512,128]{2,1,0:T(8,128)(2,1)}, f32[20,512]{1,0:T(8,128)S(1)}, f32[20,512]{1,0:T(8,128)S(1)}, s32[20]{0:T(128)S(1)}, /*index...) while((s32[]{:T(128)}, bf16[20,512,128]{2,1,0:T(8,128)(2,1)}, ...), condition=%wide.region_8.9_spmd, body=%wide.region_5.8_spmd.sunk | while | flops 68025344 | bytes 1986235 | solution.py:38
  83.3 1.2 fusion.40
  84.5 1.8 fusion.42
  89.0 1.8 fusion.42
  93.4 1.8 fusion.42
  96.6 1.2 fusion.40
  97.8 1.8 fusion.42
  101.0 1.2 fusion.40
  102.3 1.8 fusion.42
  105.4 1.2 fusion.40
  106.7 1.8 fusion.42
  111.1 1.8 fusion.42
  115.6 1.8 fusion.42
  118.7 1.2 fusion.40
  120.0 1.8 fusion.42
  124.4 1.8 fusion.42
  127.6 1.2 fusion.40
  128.8 1.8 fusion.42
  132.0 1.2 fusion.40
  133.3 1.8 fusion.42
  137.7 1.8 fusion.42
  142.1 1.8 fusion.42
  146.5 1.8 fusion.42
  151.0 1.8 fusion.42
  154.1 1.2 fusion.40
  155.4 1.8 fusion.42
  158.6 1.2 fusion.40
  159.8 1.8 fusion.42
  164.3 1.8 fusion.42
  168.7 1.8 fusion.42
  171.5 4.1 %all-to-all-start.2 = ((f32[16,1,640]{2,1,0:T(1,128)}), f32[16,1,640]{2,1,0:T(1,128)S(1)}, u32[]{:S(2)}, u32[]{:S(2)}) async-start(f32[16,1,640]{2,1,0:T(1,128)} %reshape.215), calls=%async_computation.2 | async-start | bytes 81920 | tf_op jit(solution)/shard_map/all_to_all | solution.py:53
  176.5 6.5 %all-to-all-done.2 = f32[16,1,640]{2,1,0:T(1,128)S(1)} async-done(((f32[16,1,640]{2,1,0:T(1,128)}), f32[16,1,640]{2,1,0:T(1,128)S(1)}, u32[]{:S(2)}, u32[]{:S(2)}) %all-to-all-start.2) | async-done | bytes 40992 | tf_op jit(solution)/shard_map/all_to_all | solution.py:53
  183.1 3.5 all-to-all-start.1
  186.6 3.9 %copy.18 = bf16[20,16,32,128]{3,2,0,1:T(8,128)(2,1)} copy(bf16[20,16,32,128]{3,2,1,0:T(8,128)(2,1)} %bitcast.61) | data formatting | bytes 5242880 | tf_op jit(solution)/shard_map/reshape | solution.py:51
  190.5 3.5 all-to-all-done.1
  194.0 4.4 %all-to-all-start = ((bf16[20,16,32,128]{3,2,0,1:T(8,128)(2,1)}), bf16[20,16,32,128]{3,2,0,1:T(8,128)(2,1)}, u32[]{:S(2)}, u32[]{:S(2)}) async-start(bf16[20,16,32,128]{3,2,0,1:T(8,128)(2,1)} %copy.18), calls=%async_computation | async-start | bytes 5242880 | tf_op jit(solution)/shard_map/all_to_all | solution.py:68
  201.1 46.9 %all-to-all-done = bf16[20,16,32,128]{3,2,0,1:T(8,128)(2,1)} async-done(((bf16[20,16,32,128]{3,2,0,1:T(8,128)(2,1)}), bf16[20,16,32,128]{3,2,0,1:T(8,128)(2,1)}, u32[]{:S(2)}, u32[]{:S(2)}) %all-to-all-start) | async-done | bytes 2621472 | tf_op jit(solution)/shard_map/all_to_all | solution.py:68
  248.0 4.9 %fusion.12 = f32[32,20,1,128]{3,2,1,0:T(1,128)S(1)} fusion(bf16[20,16,32,1]{1,3,0,2:T(2,128)(2,1)S(1)} %copy.26, bf16[20,16,32,128]{3,2,0,1:T(8,128)(2,1)} %all-to-all-done), kind=kOutput, calls=%fused_computation.18 | convolution fusion | flops 2621440 | bytes 2969600 | tf_op jit(solution)/shard_map/hnc,hncd->hcd/dot_general | solution.py:73
  253.9 70.8 %all-gather.4.cloned.1.call-done = bf16[512,2560]{1,0:T(8,128)(2,1)} async-done(((bf16[32,2560]{1,0:T(8,128)(2,1)}), bf16[512,2560]{1,0:T(8,128)(2,1)}) %all-gather.4.cloned.1.call-update) | async-done | bytes 2621456 | tf_op jit(solution)/shard_map/all_gather | solution.py:78
  324.7 2.8 convolution_convert_fusion
  328.4 17.1 %all-reduce.2.cloned.1.call-done = bf16[16,32,320]{2,1,0:T(8,128)(2,1)} async-done(((bf16[16,32,320]{2,1,0:T(8,128)(2,1)}), bf16[16,32,320]{2,1,0:T(8,128)(2,1)}) %all-reduce.2.cloned.1.call-update) | async-done | bytes 327696 | tf_op jit(solution)/shard_map/psum | solution.py:80
  345.5 6.8 %all-to-all-start.3 = ((bf16[16,32,320]{2,1,0:T(8,128)(2,1)}), bf16[16,32,320]{2,1,0:T(8,128)(2,1)S(1)}, u32[]{:S(2)}, u32[]{:S(2)}) async-start(bf16[16,32,320]{2,1,0:T(8,128)(2,1)} %all-reduce.2.cloned.1.call-done), calls=%async_computation.3 | async-start | bytes 786432 | tf_op jit(solution)/shard_map/all_to_all | solution.py:82
  352.3 13.0 %all-to-all-done.3 = bf16[16,32,320]{2,1,0:T(8,128)(2,1)S(1)} async-done(((bf16[16,32,320]{2,1,0:T(8,128)(2,1)}), bf16[16,32,320]{2,1,0:T(8,128)(2,1)S(1)}, u32[]{:S(2)}, u32[]{:S(2)}) %all-to-all-start.3) | async-done | bytes 327712 | tf_op jit(solution)/shard_map/all_to_all | solution.py:82
  366.1 5.3 %scatter_custom_fusion.1 = bf16[256,2560]{1,0:T(8,128)(2,1)} fusion(bf16[256,2560]{1,0:T(8,128)(2,1)} %copy.57, s32[32]{0:T(128)S(1)} %get-tuple-element.53, f32[1,32,5120]{2,1,0:T(8,128)S(1)} %reshape.161, s32[]{:T(128)} %constant.71.clone.1, s32[]{:T(128)S(6)} %select_n.87, bf16[256,2560]{1,0:T(8,128)(2,1)} %param.12, s32[1024]{0:T(1024)S(1)} %pad_clamp_fusion), kind=kCustom, calls=%fused_computation.27 | custom fusion | flops 245760 | bytes 2953732 | tf_op jit(solution)/shard_map/scatter | solution.py:87
  (142 shorter events, 38.4 us)
Async XLA Ops:
  6.5 318.2 %copy-start = (bf16[2560,320]{0,1:T(8,128)(2,1)S(1)}, bf16[2560,320]{0,1:T(8,128)(2,1)}, u32[]{:S(2)}) copy-start(bf16[2560,320]{0,1:T(8,128)(2,1)} %param.15) | copy-start | bytes 4915204
  6.5 7.3 %copy-start.1 = (bf16[256,2560]{1,0:T(8,128)(2,1)S(1)}, bf16[256,2560]{1,0:T(8,128)(2,1)}, u32[]{:S(2)}) copy-start(bf16[256,2560]{1,0:T(8,128)(2,1)} %param.9) | copy-start | bytes 3932164
  6.5 2.6 copy-start.2
  6.5 75.5 %all-gather.6.cloned.1.call-start = ((), (), s32[]{:S(2)}) async-start(), calls=%async_computation.6 | async-start | bytes 2785280 | tf_op jit(solution)/shard_map/all_gather | solution.py:49
  171.5 11.6 %all-to-all-start.2 = ((f32[16,1,640]{2,1,0:T(1,128)}), f32[16,1,640]{2,1,0:T(1,128)S(1)}, u32[]{:S(2)}, u32[]{:S(2)}) async-start(f32[16,1,640]{2,1,0:T(1,128)} %reshape.215), calls=%async_computation.2 | async-start | bytes 81920 | tf_op jit(solution)/shard_map/all_to_all | solution.py:53
  183.1 10.9 %all-to-all-start.1 = ((f32[16,1,640]{2,1,0:T(1,128)}), f32[16,1,640]{2,1,0:T(1,128)S(1)}, u32[]{:S(2)}, u32[]{:S(2)}) async-start(f32[16,1,640]{2,1,0:T(1,128)} %reshape.213), calls=%async_computation.1 | async-start | bytes 81920 | tf_op jit(solution)/shard_map/all_to_all | solution.py:60
  194.0 54.0 %all-to-all-start = ((bf16[20,16,32,128]{3,2,0,1:T(8,128)(2,1)}), bf16[20,16,32,128]{3,2,0,1:T(8,128)(2,1)}, u32[]{:S(2)}, u32[]{:S(2)}) async-start(bf16[20,16,32,128]{3,2,0,1:T(8,128)(2,1)} %copy.18), calls=%async_computation | async-start | bytes 5242880 | tf_op jit(solution)/shard_map/all_to_all | solution.py:68
  198.4 126.3 %all-gather.4.cloned.1.call-start = ((), (), s32[]{:S(2)}) async-start(), calls=%async_computation.4 | async-start | bytes 2785280 | tf_op jit(solution)/shard_map/all_gather | solution.py:78
  253.8 91.7 %all-reduce.2.cloned.1.call-start = ((), (), s32[]{:S(2)}) async-start(), calls=%async_computation.5 | async-start | bytes 786432 | tf_op jit(solution)/shard_map/psum | solution.py:80
  345.5 19.8 %all-to-all-start.3 = ((bf16[16,32,320]{2,1,0:T(8,128)(2,1)}), bf16[16,32,320]{2,1,0:T(8,128)(2,1)S(1)}, u32[]{:S(2)}, u32[]{:S(2)}) async-start(bf16[16,32,320]{2,1,0:T(8,128)(2,1)} %all-reduce.2.cloned.1.call-done), calls=%async_computation.3 | async-start | bytes 786432 | tf_op jit(solution)/shard_map/all_to_all | solution.py:82
Sparse Core Ops, SparseCore 0:
  15.3 66.7 all-gather.5
  253.9 70.6 all-gather.3
  328.5 16.8 all-reduce.1
where the time goes:
time: 380 us; the launch traced here: 378 us
  waiting for transfers between devices  225 us (59%)
  matrix products  66.3 us (17%)
  local copies, waits for them, and re-layouts  27.4 us (7%)
  starting transfers between devices  19 us (5%)
  other arithmetic  13.7 us (4%)
  loops' own time  13.6 us (4%)
  between operations  13.3 us (4%)
    all_gather x1, waiting for transfers between devices, shards(): lax.all_gather(attn, 'seq', axis=0, tiled=True)  70.8 us
    all_gather x1, waiting for transfers between devices, shards(): gathered = lax.all_gather(own_queries, 'seq', axis=0, tiled=True)  66.8 us
    all_to_all x1, waiting for transfers between devices, shards(): lax.all_to_all(for_sending(block_out), 'seq', split_axis=1, concat_axis=1...  46.9 us
    dot_general x20, matrix products, one_head(): jnp.dot(expo.astype(jnp.bfloat16), v_head, preferred_element_type=jnp.flo...  35.6 us
    dot_general x20, matrix products, one_head(): lax.dot_general(q_head, k_head, (((1,), (1,)), ((), ())), preferred_eleme...  23 us
    psum x1, waiting for transfers between devices, shards(): terms = lax.psum(terms.astype(jnp.bfloat16), 'head').astype(jnp.float32)  17.1 us
    another operation x1, loops' own time, local_partials(): return lax.map(one_head, jnp.arange(head_count, dtype=jnp.int32))  13.6 us
    all_to_all x1, waiting for transfers between devices, shards(): lax.all_to_all(terms.astype(jnp.bfloat16), 'seq', split_axis=0, concat_ax...  13 us
  transfers between devices with their start and end apart: 7, of which 7 were waited for; matrix products, arithmetic and copies ran while one was open for 2% of the time, Pallas kernels for 0%

commit v1 on v0

--- a/solution.py
+++ b/solution.py
@@ -1,9 +1,25 @@
+import functools
 import jax
 import jax.numpy as jnp
 from jax import lax
 from jax.sharding import PartitionSpec as P
 
 HD = 128
+
+
+def make_patch_for(arr, k_dim):
+    n = lax.axis_size("seq")
+    extra = [(k0 - 1, k0) for k0 in range(1, n)] + [(n - 1, 0)]
+    plain = arr
+    line_up = [plain]
+    for _ in range(n - 1):
+        plain = lax.ppermute(plain, "seq", extra)
+        line_up += [plain]
+    all_values = jnp.concatenate([*reversed(line_up)], axis=k_dim)
+    return jnp.roll(all_values, (lax.axis_index("seq") + 1) * plain.shape[k_dim], axis=k_dim)
+
+
+joints_pass = functools.partial(make_patch_for, k_dim=0)
 
 
 def for_sending(value):
@@ -46,7 +62,7 @@
     act_rows = jnp.nonzero(active, size=capacity, fill_value=tok_dev)[0].astype(jnp.int32)
     safe_rows = jnp.minimum(act_rows, tok_dev - 1)
     own_queries = queries[safe_rows]
-    gathered = lax.all_gather(own_queries, "seq", axis=0, tiled=True)
+    gathered = joints_pass(own_queries)
     block_out, block_peak, block_total = local_partials(gathered, keys, values)
     block_out = block_out.reshape(head_count, devices, capacity, HD)
     peak_in, total_in = (

time: 380 us -> 452 us (1.19)
  waiting for transfers between devices: 225 us -> 276 us
  local copies, waits for them, and re-layouts: 27.4 us -> 39.7 us
  starting transfers between devices: 19 us -> 24.7 us
    ppermute x0 -> x15, waiting for transfers between devices: none -> 136 us  [make_patch_for(): plain = lax.ppermute(plain, 'seq', extra)]
    all_gather x1 -> x0, waiting for transfers between devices: 66.8 us -> none  [shards(): gathered = lax.all_gather(own_queries, 'seq', axis=0, tiled=True)]
    all_to_all x1, waiting for transfers between devices: 46.9 us -> 33.2 us  [shards(): lax.all_to_all(for_sending(block_out), 'seq', split_axis=1, concat_axis=1...]
    unnamed x12 -> x51, local copies, waits for them, and re-layouts: 4.98 us -> 13.7 us
  transfers between devices with their start and end apart: 7 -> 21, of which waited for: 7 -> 21; matrix products, arithmetic and copies ran while one was open for 2% -> 2% of each run, Pallas kernels for 0% -> 0%
where the time goes in v1:
time: 452 us; the launch traced here: 450 us
  waiting for transfers between devices  276 us (61%)
  matrix products  66.4 us (15%)
  local copies, waits for them, and re-layouts  39.7 us (9%)
  starting transfers between devices  24.7 us (5%)
  other arithmetic  15 us (3%)
  between operations  13.9 us (3%)
  loops' own time  13.6 us (3%)
    ppermute x15, waiting for transfers between devices, make_patch_for(): plain = lax.ppermute(plain, 'seq', extra)  136 us
    all_gather x1, waiting for transfers between devices, shards(): lax.all_gather(attn, 'seq', axis=0, tiled=True)  66.7 us
    dot_general x20, matrix products, one_head(): jnp.dot(expo.astype(jnp.bfloat16), v_head, preferred_element_type=jnp.flo...  35.6 us
    all_to_all x1, waiting for transfers between devices, shards(): lax.all_to_all(for_sending(block_out), 'seq', split_axis=1, concat_axis=1...  33.2 us
    dot_general x20, matrix products, one_head(): lax.dot_general(q_head, k_head, (((1,), (1,)), ((), ())), preferred_eleme...  23 us
    psum x1, waiting for transfers between devices, shards(): terms = lax.psum(terms.astype(jnp.bfloat16), 'head').astype(jnp.float32)  17 us
    unnamed x51, local copies, waits for them, and re-layouts  13.7 us
    another operation x1, loops' own time, local_partials(): return lax.map(one_head, jnp.arange(head_count, dtype=jnp.int32))  13.6 us
  transfers between devices with their start and end apart: 21, of which 21 were waited for; matrix products, arithmetic and copies ran while one was open for 2% of the time, Pallas kernels for 0%

profile of v1, /device:TPU:0, one launch (start us, length us, event | category | flops | bytes accessed | tf_op | source)
XLA Modules:
  0.0 449.5 jit_solution(14568617575904556824)
XLA Ops:
  6.5 2.6 copy.88
  11.8 2.3 scatter_custom_fusion
  15.1 2.3 gather_fusion
  17.4 3.0 collective-permute-start
  20.4 8.2 %collective-permute-done = bf16[32,2560]{1,0:T(8,128)(2,1)S(1)} collective-permute-done((bf16[32,2560]{1,0:T(8,128)(2,1)S(1)}, bf16[32,2560]{1,0:T(8,128)(2,1)S(1)}, u32[]{:S(2)}, u32[]{:S(2)}) %collective-permute-start) | collective-permute-done | bytes 163872 | tf_op jit(solution)/shard_map/ppermute | solution.py:16
  28.6 9.0 %collective-permute-done.1 = bf16[32,2560]{1,0:T(8,128)(2,1)S(1)} collective-permute-done((bf16[32,2560]{1,0:T(8,128)(2,1)S(1)}, bf16[32,2560]{1,0:T(8,128)(2,1)S(1)}, u32[]{:S(2)}, u32[]{:S(2)}) %collective-permute-start.1) | collective-permute-done | bytes 163872 | tf_op jit(solution)/shard_map/ppermute | solution.py:16
  37.6 8.9 %collective-permute-done.2 = bf16[32,2560]{1,0:T(8,128)(2,1)S(1)} collective-permute-done((bf16[32,2560]{1,0:T(8,128)(2,1)S(1)}, bf16[32,2560]{1,0:T(8,128)(2,1)S(1)}, u32[]{:S(2)}, u32[]{:S(2)}) %collective-permute-start.2) | collective-permute-done | bytes 163872 | tf_op jit(solution)/shard_map/ppermute | solution.py:16
  46.5 8.9 %collective-permute-done.3 = bf16[32,2560]{1,0:T(8,128)(2,1)S(1)} collective-permute-done((bf16[32,2560]{1,0:T(8,128)(2,1)S(1)}, bf16[32,2560]{1,0:T(8,128)(2,1)S(1)}, u32[]{:S(2)}, u32[]{:S(2)}) %collective-permute-start.3) | collective-permute-done | bytes 163872 | tf_op jit(solution)/shard_map/ppermute | solution.py:16
  55.4 8.9 %collective-permute-done.4 = bf16[32,2560]{1,0:T(8,128)(2,1)S(1)} collective-permute-done((bf16[32,2560]{1,0:T(8,128)(2,1)S(1)}, bf16[32,2560]{1,0:T(8,128)(2,1)S(1)}, u32[]{:S(2)}, u32[]{:S(2)}) %collective-permute-start.4) | collective-permute-done | bytes 163872 | tf_op jit(solution)/shard_map/ppermute | solution.py:16
  64.3 8.9 %collective-permute-done.5 = bf16[32,2560]{1,0:T(8,128)(2,1)S(1)} collective-permute-done((bf16[32,2560]{1,0:T(8,128)(2,1)S(1)}, bf16[32,2560]{1,0:T(8,128)(2,1)S(1)}, u32[]{:S(2)}, u32[]{:S(2)}) %collective-permute-start.5) | collective-permute-done | bytes 163872 | tf_op jit(solution)/shard_map/ppermute | solution.py:16
  73.2 10.1 %collective-permute-done.6 = bf16[32,2560]{1,0:T(8,128)(2,1)S(1)} collective-permute-done((bf16[32,2560]{1,0:T(8,128)(2,1)S(1)}, bf16[32,2560]{1,0:T(8,128)(2,1)S(1)}, u32[]{:S(2)}, u32[]{:S(2)}) %collective-permute-start.6) | collective-permute-done | bytes 163872 | tf_op jit(solution)/shard_map/ppermute | solution.py:16
  83.3 10.1 %collective-permute-done.7 = bf16[32,2560]{1,0:T(8,128)(2,1)S(1)} collective-permute-done((bf16[32,2560]{1,0:T(8,128)(2,1)S(1)}, bf16[32,2560]{1,0:T(8,128)(2,1)S(1)}, u32[]{:S(2)}, u32[]{:S(2)}) %collective-permute-start.7) | collective-permute-done | bytes 163872 | tf_op jit(solution)/shard_map/ppermute | solution.py:16
  93.4 9.3 %collective-permute-done.8 = bf16[32,2560]{1,0:T(8,128)(2,1)S(1)} collective-permute-done((bf16[32,2560]{1,0:T(8,128)(2,1)S(1)}, bf16[32,2560]{1,0:T(8,128)(2,1)S(1)}, u32[]{:S(2)}, u32[]{:S(2)}) %collective-permute-start.8) | collective-permute-done | bytes 163872 | tf_op jit(solution)/shard_map/ppermute | solution.py:16
  102.7 8.9 %collective-permute-done.9 = bf16[32,2560]{1,0:T(8,128)(2,1)S(1)} collective-permute-done((bf16[32,2560]{1,0:T(8,128)(2,1)S(1)}, bf16[32,2560]{1,0:T(8,128)(2,1)S(1)}, u32[]{:S(2)}, u32[]{:S(2)}) %collective-permute-start.9) | collective-permute-done | bytes 163872 | tf_op jit(solution)/shard_map/ppermute | solution.py:16
  111.6 8.9 %collective-permute-done.10 = bf16[32,2560]{1,0:T(8,128)(2,1)S(1)} collective-permute-done((bf16[32,2560]{1,0:T(8,128)(2,1)S(1)}, bf16[32,2560]{1,0:T(8,128)(2,1)S(1)}, u32[]{:S(2)}, u32[]{:S(2)}) %collective-permute-start.10) | collective-permute-done | bytes 163872 | tf_op jit(solution)/shard_map/ppermute | solution.py:16
  121.2 8.9 %collective-permute-done.11 = bf16[32,2560]{1,0:T(8,128)(2,1)S(1)} collective-permute-done((bf16[32,2560]{1,0:T(8,128)(2,1)S(1)}, bf16[32,2560]{1,0:T(8,128)(2,1)S(1)}, u32[]{:S(2)}, u32[]{:S(2)}) %collective-permute-start.11) | collective-permute-done | bytes 163872 | tf_op jit(solution)/shard_map/ppermute | solution.py:16
  130.8 8.9 %collective-permute-done.12 = bf16[32,2560]{1,0:T(8,128)(2,1)S(1)} collective-permute-done((bf16[32,2560]{1,0:T(8,128)(2,1)S(1)}, bf16[32,2560]{1,0:T(8,128)(2,1)S(1)}, u32[]{:S(2)}, u32[]{:S(2)}) %collective-permute-start.12) | collective-permute-done | bytes 163872 | tf_op jit(solution)/shard_map/ppermute | solution.py:16
  140.3 9.0 %collective-permute-done.13 = bf16[32,2560]{1,0:T(8,128)(2,1)} collective-permute-done((bf16[32,2560]{1,0:T(8,128)(2,1)S(1)}, bf16[32,2560]{1,0:T(8,128)(2,1)}, u32[]{:S(2)}, u32[]{:S(2)}) %collective-permute-start.13) | collective-permute-done | bytes 163872 | tf_op jit(solution)/shard_map/ppermute | solution.py:16
  149.4 9.2 %collective-permute-done.14 = bf16[32,2560]{1,0:T(8,128)(2,1)} collective-permute-done((bf16[32,2560]{1,0:T(8,128)(2,1)}, bf16[32,2560]{1,0:T(8,128)(2,1)}, u32[]{:S(2)}, u32[]{:S(2)}) %collective-permute-start.14) | collective-permute-done | bytes 163872 | tf_op jit(solution)/shard_map/ppermute | solution.py:16
  167.3 89.4 %while.14 = (s32[]{:T(128)}, bf16[20,512,128]{2,1,0:T(8,128)(2,1)}, f32[20,512]{1,0:T(8,128)S(1)}, f32[20,512]{1,0:T(8,128)S(1)}, s32[20]{0:T(128)S(1)}, /*index...) while((s32[]{:T(128)}, bf16[20,512,128]{2,1,0:T(8,128)(2,1)}, ...), condition=%wide.region_8.9_spmd, body=%wide.region_5.8_spmd.sunk | while | flops 68025344 | bytes 1986235 | solution.py:54
  174.4 1.8 fusion.42
  178.9 1.8 fusion.42
  183.3 1.8 fusion.42
  187.8 1.8 fusion.42
  192.3 1.8 fusion.42
  196.7 1.8 fusion.42
  210.1 1.8 fusion.42
  219.1 1.8 fusion.42
  232.5 1.8 fusion.42
  237.0 1.8 fusion.42
  241.4 1.8 fusion.42
  245.9 1.8 fusion.42
  250.4 1.8 fusion.42
  254.9 1.8 fusion.42
  257.7 3.5 all-to-all-start.2
  262.1 6.6 %all-to-all-done.2 = f32[16,1,640]{2,1,0:T(1,128)S(1)} async-done(((f32[16,1,640]{2,1,0:T(1,128)}), f32[16,1,640]{2,1,0:T(1,128)S(1)}, u32[]{:S(2)}, u32[]{:S(2)}) %all-to-all-start.2) | async-done | bytes 40992 | tf_op jit(solution)/shard_map/all_to_all | solution.py:69
  268.7 3.5 all-to-all-start.1
  272.2 3.9 copy.18
  276.1 3.6 all-to-all-done.1
  279.7 7.6 %all-to-all-start = ((bf16[20,16,32,128]{3,2,0,1:T(8,128)(2,1)}), bf16[20,16,32,128]{3,2,0,1:T(8,128)(2,1)}, u32[]{:S(2)}, u32[]{:S(2)}) async-start(bf16[20,16,32,128]{3,2,0,1:T(8,128)(2,1)} %copy.18), calls=%async_computation | async-start | bytes 5242880 | tf_op jit(solution)/shard_map/all_to_all | solution.py:84
  290.1 33.2 %all-to-all-done = bf16[20,16,32,128]{3,2,0,1:T(8,128)(2,1)} async-done(((bf16[20,16,32,128]{3,2,0,1:T(8,128)(2,1)}), bf16[20,16,32,128]{3,2,0,1:T(8,128)(2,1)}, u32[]{:S(2)}, u32[]{:S(2)}) %all-to-all-start) | async-done | bytes 2621472 | tf_op jit(solution)/shard_map/all_to_all | solution.py:84
  323.3 4.9 %fusion.12 = f32[32,20,1,128]{3,2,1,0:T(1,128)S(1)} fusion(bf16[20,16,32,1]{1,3,0,2:T(2,128)(2,1)S(1)} %copy.26, bf16[20,16,32,128]{3,2,0,1:T(8,128)(2,1)} %all-to-all-done), kind=kOutput, calls=%fused_computation.18 | convolution fusion | flops 2621440 | bytes 2969600 | tf_op jit(solution)/shard_map/hnc,hncd->hcd/dot_general | solution.py:89
  329.3 66.7 %all-gather.2.cloned.1.call-done = bf16[512,2560]{1,0:T(8,128)(2,1)} async-done(((bf16[32,2560]{1,0:T(8,128)(2,1)}), bf16[512,2560]{1,0:T(8,128)(2,1)}) %all-gather.2.cloned.1.call-update) | async-done | bytes 2621456 | tf_op jit(solution)/shard_map/all_gather | solution.py:94
  396.0 2.8 convolution_convert_fusion
  399.7 17.0 %all-reduce.2.cloned.1.call-done = bf16[16,32,320]{2,1,0:T(8,128)(2,1)} async-done(((bf16[16,32,320]{2,1,0:T(8,128)(2,1)}), bf16[16,32,320]{2,1,0:T(8,128)(2,1)}) %all-reduce.2.cloned.1.call-update) | async-done | bytes 327696 | tf_op jit(solution)/shard_map/psum | solution.py:96
  416.8 6.8 %all-to-all-start.3 = ((bf16[16,32,320]{2,1,0:T(8,128)(2,1)}), bf16[16,32,320]{2,1,0:T(8,128)(2,1)S(1)}, u32[]{:S(2)}, u32[]{:S(2)}) async-start(bf16[16,32,320]{2,1,0:T(8,128)(2,1)} %all-reduce.2.cloned.1.call-done), calls=%async_computation.3 | async-start | bytes 786432 | tf_op jit(solution)/shard_map/all_to_all | solution.py:98
  423.6 13.0 %all-to-all-done.3 = bf16[16,32,320]{2,1,0:T(8,128)(2,1)S(1)} async-done(((bf16[16,32,320]{2,1,0:T(8,128)(2,1)}), bf16[16,32,320]{2,1,0:T(8,128)(2,1)S(1)}, u32[]{:S(2)}, u32[]{:S(2)}) %all-to-all-start.3) | async-done | bytes 327712 | tf_op jit(solution)/shard_map/all_to_all | solution.py:98
  437.4 5.3 %scatter_custom_fusion.1 = bf16[256,2560]{1,0:T(8,128)(2,1)} fusion(bf16[256,2560]{1,0:T(8,128)(2,1)} %copy.88, s32[32]{0:T(128)S(1)} %get-tuple-element.53, f32[1,32,5120]{2,1,0:T(8,128)S(1)} %reshape.161, s32[]{:T(128)} %constant.93.clone.1, s32[]{:T(128)S(6)} %select_n.101, bf16[256,2560]{1,0:T(8,128)(2,1)} %param.12, s32[1024]{0:T(1024)S(1)} %pad_clamp_fusion), kind=kCustom, calls=%fused_computation.27 | custom fusion | flops 245760 | bytes 2953732 | tf_op jit(solution)/shard_map/scatter | solution.py:103
  (210 shorter events, 72.3 us)
Async XLA Ops:
  6.5 389.4 %copy-start = (bf16[2560,320]{0,1:T(8,128)(2,1)S(1)}, bf16[2560,320]{0,1:T(8,128)(2,1)}, u32[]{:S(2)}) copy-start(bf16[2560,320]{0,1:T(8,128)(2,1)} %param.15) | copy-start | bytes 4915204
  17.4 11.2 %collective-permute-start = (bf16[32,2560]{1,0:T(8,128)(2,1)S(1)}, bf16[32,2560]{1,0:T(8,128)(2,1)S(1)}, u32[]{:S(2)}, u32[]{:S(2)}) collective-permute-start(bf16[32,2560]{1,0:T(8,128)(2,1)S(1)} %gather_fusion), channel_id=1, source_target_pairs={{0,2},{2,4},{4,6},{6,8},{8,10},{10,12},{12,14},{14,16},{16,18},{18... | collective-permute-start | bytes 491528 | tf_op jit(solution)/shard_map/ppermute | solution.py:16
  28.6 9.0 %collective-permute-start.1 = (bf16[32,2560]{1,0:T(8,128)(2,1)S(1)}, bf16[32,2560]{1,0:T(8,128)(2,1)S(1)}, u32[]{:S(2)}, u32[]{:S(2)}) collective-permute-start(bf16[32,2560]{1,0:T(8,128)(2,1)S(1)} %collective-permute-done), channel_id=1, source_target_pairs={{0,2},{2,4},{4,6},{6,8},{8,10},{10,12},{12,14},{14,16},{16,18},{18... | collective-permute-start | bytes 491528 | tf_op jit(solution)/shard_map/ppermute | solution.py:16
  37.6 8.9 %collective-permute-start.2 = (bf16[32,2560]{1,0:T(8,128)(2,1)S(1)}, bf16[32,2560]{1,0:T(8,128)(2,1)S(1)}, u32[]{:S(2)}, u32[]{:S(2)}) collective-permute-start(bf16[32,2560]{1,0:T(8,128)(2,1)S(1)} %collective-permute-done.1), channel_id=1, source_target_pairs={{0,2},{2,4},{4,6},{6,8},{8,10},{10,12},{12,14},{14,16},{16,18},{18... | collective-permute-start | bytes 491528 | tf_op jit(solution)/shard_map/ppermute | solution.py:16
  46.5 8.9 %collective-permute-start.3 = (bf16[32,2560]{1,0:T(8,128)(2,1)S(1)}, bf16[32,2560]{1,0:T(8,128)(2,1)S(1)}, u32[]{:S(2)}, u32[]{:S(2)}) collective-permute-start(bf16[32,2560]{1,0:T(8,128)(2,1)S(1)} %collective-permute-done.2), channel_id=1, source_target_pairs={{0,2},{2,4},{4,6},{6,8},{8,10},{10,12},{12,14},{14,16},{16,18},{18... | collective-permute-start | bytes 491528 | tf_op jit(solution)/shard_map/ppermute | solution.py:16
  55.4 8.9 %collective-permute-start.4 = (bf16[32,2560]{1,0:T(8,128)(2,1)S(1)}, bf16[32,2560]{1,0:T(8,128)(2,1)S(1)}, u32[]{:S(2)}, u32[]{:S(2)}) collective-permute-start(bf16[32,2560]{1,0:T(8,128)(2,1)S(1)} %collective-permute-done.3), channel_id=1, source_target_pairs={{0,2},{2,4},{4,6},{6,8},{8,10},{10,12},{12,14},{14,16},{16,18},{18... | collective-permute-start | bytes 491528 | tf_op jit(solution)/shard_map/ppermute | solution.py:16
  64.3 8.9 %collective-permute-start.5 = (bf16[32,2560]{1,0:T(8,128)(2,1)S(1)}, bf16[32,2560]{1,0:T(8,128)(2,1)S(1)}, u32[]{:S(2)}, u32[]{:S(2)}) collective-permute-start(bf16[32,2560]{1,0:T(8,128)(2,1)S(1)} %collective-permute-done.4), channel_id=1, source_target_pairs={{0,2},{2,4},{4,6},{6,8},{8,10},{10,12},{12,14},{14,16},{16,18},{18... | collective-permute-start | bytes 491528 | tf_op jit(solution)/shard_map/ppermute | solution.py:16
  73.2 10.1 %collective-permute-start.6 = (bf16[32,2560]{1,0:T(8,128)(2,1)S(1)}, bf16[32,2560]{1,0:T(8,128)(2,1)S(1)}, u32[]{:S(2)}, u32[]{:S(2)}) collective-permute-start(bf16[32,2560]{1,0:T(8,128)(2,1)S(1)} %collective-permute-done.5), channel_id=1, source_target_pairs={{0,2},{2,4},{4,6},{6,8},{8,10},{10,12},{12,14},{14,16},{16,18},{18... | collective-permute-start | bytes 491528 | tf_op jit(solution)/shard_map/ppermute | solution.py:16
  83.3 10.1 %collective-permute-start.7 = (bf16[32,2560]{1,0:T(8,128)(2,1)S(1)}, bf16[32,2560]{1,0:T(8,128)(2,1)S(1)}, u32[]{:S(2)}, u32[]{:S(2)}) collective-permute-start(bf16[32,2560]{1,0:T(8,128)(2,1)S(1)} %collective-permute-done.6), channel_id=1, source_target_pairs={{0,2},{2,4},{4,6},{6,8},{8,10},{10,12},{12,14},{14,16},{16,18},{18... | collective-permute-start | bytes 491528 | tf_op jit(solution)/shard_map/ppermute | solution.py:16
  93.4 9.3 %collective-permute-start.8 = (bf16[32,2560]{1,0:T(8,128)(2,1)S(1)}, bf16[32,2560]{1,0:T(8,128)(2,1)S(1)}, u32[]{:S(2)}, u32[]{:S(2)}) collective-permute-start(bf16[32,2560]{1,0:T(8,128)(2,1)S(1)} %collective-permute-done.7), channel_id=1, source_target_pairs={{0,2},{2,4},{4,6},{6,8},{8,10},{10,12},{12,14},{14,16},{16,18},{18... | collective-permute-start | bytes 491528 | tf_op jit(solution)/shard_map/ppermute | solution.py:16
  102.7 8.9 %collective-permute-start.9 = (bf16[32,2560]{1,0:T(8,128)(2,1)S(1)}, bf16[32,2560]{1,0:T(8,128)(2,1)S(1)}, u32[]{:S(2)}, u32[]{:S(2)}) collective-permute-start(bf16[32,2560]{1,0:T(8,128)(2,1)S(1)} %collective-permute-done.8), channel_id=1, source_target_pairs={{0,2},{2,4},{4,6},{6,8},{8,10},{10,12},{12,14},{14,16},{16,18},{18... | collective-permute-start | bytes 491528 | tf_op jit(solution)/shard_map/ppermute | solution.py:16
  111.6 8.9 %collective-permute-start.10 = (bf16[32,2560]{1,0:T(8,128)(2,1)S(1)}, bf16[32,2560]{1,0:T(8,128)(2,1)S(1)}, u32[]{:S(2)}, u32[]{:S(2)}) collective-permute-start(bf16[32,2560]{1,0:T(8,128)(2,1)S(1)} %collective-permute-done.9), channel_id=1, source_target_pairs={{0,2},{2,4},{4,6},{6,8},{8,10},{10,12},{12,14},{14,16},{16,18},{18... | collective-permute-start | bytes 491528 | tf_op jit(solution)/shard_map/ppermute | solution.py:16
  120.5 0.7 copy-start.1
  121.2 8.9 %collective-permute-start.11 = (bf16[32,2560]{1,0:T(8,128)(2,1)S(1)}, bf16[32,2560]{1,0:T(8,128)(2,1)S(1)}, u32[]{:S(2)}, u32[]{:S(2)}) collective-permute-start(bf16[32,2560]{1,0:T(8,128)(2,1)S(1)} %collective-permute-done.10), channel_id=1, source_target_pairs={{0,2},{2,4},{4,6},{6,8},{8,10},{10,12},{12,14},{14,16},{16,18},{18... | collective-permute-start | bytes 491528 | tf_op jit(solution)/shard_map/ppermute | solution.py:16
  130.1 0.7 copy-start.3
  130.8 8.9 %collective-permute-start.12 = (bf16[32,2560]{1,0:T(8,128)(2,1)S(1)}, bf16[32,2560]{1,0:T(8,128)(2,1)S(1)}, u32[]{:S(2)}, u32[]{:S(2)}) collective-permute-start(bf16[32,2560]{1,0:T(8,128)(2,1)S(1)} %collective-permute-done.11), channel_id=1, source_target_pairs={{0,2},{2,4},{4,6},{6,8},{8,10},{10,12},{12,14},{14,16},{16,18},{18... | collective-permute-start | bytes 491528 | tf_op jit(solution)/shard_map/ppermute | solution.py:16
  139.7 0.7 copy-start.5
  140.3 9.0 %collective-permute-start.13 = (bf16[32,2560]{1,0:T(8,128)(2,1)S(1)}, bf16[32,2560]{1,0:T(8,128)(2,1)}, u32[]{:S(2)}, u32[]{:S(2)}) collective-permute-start(bf16[32,2560]{1,0:T(8,128)(2,1)S(1)} %collective-permute-done.12), channel_id=1, source_target_pairs={{0,2},{2,4},{4,6},{6,8},{8,10},{10,12},{12,14},{14,16},{16,18},{18... | collective-permute-start | bytes 491528 | tf_op jit(solution)/shard_map/ppermute | solution.py:16
  149.4 9.2 %collective-permute-start.14 = (bf16[32,2560]{1,0:T(8,128)(2,1)}, bf16[32,2560]{1,0:T(8,128)(2,1)}, u32[]{:S(2)}, u32[]{:S(2)}) collective-permute-start(bf16[32,2560]{1,0:T(8,128)(2,1)} %collective-permute-done.13), channel_id=1, source_target_pairs={{0,2},{2,4},{4,6},{6,8},{8,10},{10,12},{12,14},{14,16},{16,18},{18... | collective-permute-start | bytes 491528 | tf_op jit(solution)/shard_map/ppermute | solution.py:16
  149.4 16.0 %copy-start.6 = (bf16[32,2560]{1,0:T(8,128)(2,1)S(1)}, bf16[32,2560]{1,0:T(8,128)(2,1)}, u32[]{:S(2)}) copy-start(bf16[32,2560]{1,0:T(8,128)(2,1)} %copy-done.5) | copy-start | bytes 491524
  149.4 16.0 %copy-start.4 = (bf16[32,2560]{1,0:T(8,128)(2,1)S(1)}, bf16[32,2560]{1,0:T(8,128)(2,1)}, u32[]{:S(2)}) copy-start(bf16[32,2560]{1,0:T(8,128)(2,1)} %copy-done.3) | copy-start | bytes 491524
  149.4 16.0 %copy-start.2 = (bf16[32,2560]{1,0:T(8,128)(2,1)S(1)}, bf16[32,2560]{1,0:T(8,128)(2,1)}, u32[]{:S(2)}) copy-start(bf16[32,2560]{1,0:T(8,128)(2,1)} %copy-done.1) | copy-start | bytes 491524
  257.7 11.0 %all-to-all-start.2 = ((f32[16,1,640]{2,1,0:T(1,128)}), f32[16,1,640]{2,1,0:T(1,128)S(1)}, u32[]{:S(2)}, u32[]{:S(2)}) async-start(f32[16,1,640]{2,1,0:T(1,128)} %reshape.214), calls=%async_computation.2 | async-start | bytes 81920 | tf_op jit(solution)/shard_map/all_to_all | solution.py:69
  268.7 11.1 %all-to-all-start.1 = ((f32[16,1,640]{2,1,0:T(1,128)}), f32[16,1,640]{2,1,0:T(1,128)S(1)}, u32[]{:S(2)}, u32[]{:S(2)}) async-start(f32[16,1,640]{2,1,0:T(1,128)} %reshape.212), calls=%async_computation.1 | async-start | bytes 81920 | tf_op jit(solution)/shard_map/all_to_all | solution.py:76
  279.7 43.5 %all-to-all-start = ((bf16[20,16,32,128]{3,2,0,1:T(8,128)(2,1)}), bf16[20,16,32,128]{3,2,0,1:T(8,128)(2,1)}, u32[]{:S(2)}, u32[]{:S(2)}) async-start(bf16[20,16,32,128]{3,2,0,1:T(8,128)(2,1)} %copy.18), calls=%async_computation | async-start | bytes 5242880 | tf_op jit(solution)/shard_map/all_to_all | solution.py:84
  287.4 108.6 %all-gather.2.cloned.1.call-start = ((), (), s32[]{:S(2)}) async-start(), calls=%async_computation.4 | async-start | bytes 2785280 | tf_op jit(solution)/shard_map/all_gather | solution.py:94
  329.1 87.7 %all-reduce.2.cloned.1.call-start = ((), (), s32[]{:S(2)}) async-start(), calls=%async_computation.5 | async-start | bytes 786432 | tf_op jit(solution)/shard_map/psum | solution.py:96
  416.8 19.8 %all-to-all-start.3 = ((bf16[16,32,320]{2,1,0:T(8,128)(2,1)}), bf16[16,32,320]{2,1,0:T(8,128)(2,1)S(1)}, u32[]{:S(2)}, u32[]{:S(2)}) async-start(bf16[16,32,320]{2,1,0:T(8,128)(2,1)} %all-reduce.2.cloned.1.call-done), calls=%async_computation.3 | async-start | bytes 786432 | tf_op jit(solution)/shard_map/all_to_all | solution.py:98
Sparse Core Ops, SparseCore 0:
  329.2 66.7 all-gather.1
  399.8 16.8 all-reduce.1
